TPU v7x, 256 devices: a whole 4x4x8 slice. The times are simulated.
256 devices in a mesh: seq: 32 (over z, x), head: 8 (over y, core).
Axes of the slice: x: 4, y: 4, z: 8, core: 2. Of those that a mesh axis runs over, the one named last changes fastest.
Arguments:
- queries: bfloat16 [65536, 8192], P(('seq', 'head')), may hold values from -50 to 50
- keys: bfloat16 [65536, 1024], P(('seq', 'head')), may hold values from -6 to 6
- values: bfloat16 [65536, 1024], P(('seq', 'head')), may hold values from -15 to 15
- pattern: int32 [512, 16], replicated, may hold values from 0 to 510, as said below
- keep: int32 [512, 16], replicated, may hold values from 0 to 1, as said below
Outputs:
- attended: bfloat16 [65536, 8192], P(('seq', 'head'))
Inputs may be any that keep to these rules, and one draw needn't show every extreme that they name: `pattern`: entry b of query block i's list is i - 1 for b = 0; for b >= 1 it is i - 2^b or i - 2^b with its lowest bit flipped; it is 0 wherever i < 2^b. `keep`: 0 wherever i < 2^b.
All inputs are finite; a program needn't handle non-finite values.
Results may differ from a plain program's by a relative error of at most 0.0049.
Values may be sent and summed in bfloat16 or wider, within the bound.
A program may use at most 128 MiB of HBM per device.

v0:
```python
import math

import jax
import jax.numpy as jnp
from jax import lax
from jax.sharding import PartitionSpec as P

QUERY_HEADS = 64
KEY_VALUE_HEADS = 8
HEAD_SIZE = 128
BLOCK_TOKENS = 128


def shifted(x, axis, by):
    count = lax.axis_size(axis)
    pairs = [(i, i + by) for i in range(count) if 0 <= i + by < count]
    return lax.ppermute(x, axis, pairs)


def unit_attend(operands):
    query_unit, pair_unit, live_unit = operands
    slot_count = live_unit.shape[1]
    score_scale = 1.0 / math.sqrt(query_unit.shape[-1])
    scores = (
        jnp.einsum("gqrd,glpd->grqlp", query_unit, pair_unit[0], preferred_element_type=jnp.float32)
        * score_scale
    )
    causal = jnp.arange(BLOCK_TOKENS)[:, None] >= jnp.arange(BLOCK_TOKENS)[None, :]
    diag_slot = jnp.arange(slot_count) == 0
    allowed = jnp.where(
        diag_slot[None, None, None, :, None],
        causal[None, None, :, None, :],
        (live_unit > 0)[:, None, None, :, None],
    )
    scores = jnp.where(allowed, scores, -1e30)
    peak = jnp.max(scores, axis=(3, 4), keepdims=True)
    expo = jnp.exp(scores - peak)
    weights = (expo / jnp.sum(expo, axis=(3, 4), keepdims=True)).astype(jnp.bfloat16)
    result = jnp.einsum(
        "grqlp,glpd->gqrd", weights, pair_unit[1], preferred_element_type=jnp.float32
    )
    return result.astype(jnp.bfloat16)


def attend(query_rows, kv_pair, pattern, keep, fetch_blocks, place, count):
    row_count = query_rows.shape[0]
    nb_local = row_count // BLOCK_TOKENS
    width = kv_pair.shape[1]
    kv_local = width // (2 * HEAD_SIZE)
    group_width = QUERY_HEADS // KEY_VALUE_HEADS
    nb_total = nb_local * count
    levels = (nb_total - 1).bit_length()
    fetched = {}
    for bit_index in range(count.bit_length() - 1):
        distance = 2**bit_index
        fetched[distance] = fetch_blocks(kv_pair, distance).reshape(nb_local, BLOCK_TOKENS, width)
    own_blocks = kv_pair.reshape(nb_local, BLOCK_TOKENS, width)
    near_blocks = jnp.concatenate([fetched[1], own_blocks], 0)
    first_row = place * nb_local
    pattern_rows = lax.dynamic_slice_in_dim(pattern, first_row, nb_local, 0)
    keep_rows = lax.dynamic_slice_in_dim(keep, first_row, nb_local, 0)
    chosen = [own_blocks]
    for level_index in range(levels):
        span_blocks = 2**level_index
        if span_blocks < nb_local:
            source = near_blocks
            base_block = (place - 1) * nb_local
        else:
            shift_by = span_blocks // nb_local
            source = fetched[shift_by]
            base_block = (place - shift_by) * nb_local
        local_index = jnp.clip(pattern_rows[:, level_index] - base_block, 0, source.shape[0] - 1)
        chosen.append(jnp.take(source, local_index, axis=0))
    keyset = jnp.stack(chosen, 1)
    live_slots = jnp.concatenate([jnp.ones((nb_local, 1), jnp.int32), keep_rows[:, :levels]], 1)
    group_blocks = min(nb_local, max(1, 2048 // (BLOCK_TOKENS * group_width)))
    block_groups = nb_local // group_blocks
    units = block_groups * kv_local
    query_units = query_rows.reshape(
        block_groups, group_blocks, BLOCK_TOKENS, kv_local, group_width, HEAD_SIZE
    )
    query_units = query_units.transpose(0, 3, 1, 2, 4, 5).reshape(
        units, group_blocks, BLOCK_TOKENS, group_width, HEAD_SIZE
    )
    pair_units = keyset.reshape(
        block_groups, group_blocks, levels + 1, BLOCK_TOKENS, 2, kv_local, HEAD_SIZE
    )
    pair_units = pair_units.transpose(0, 5, 4, 1, 2, 3, 6).reshape(
        units, 2, group_blocks, levels + 1, BLOCK_TOKENS, HEAD_SIZE
    )
    live_units = jnp.broadcast_to(
        live_slots.reshape(block_groups, 1, group_blocks, levels + 1),
        (block_groups, kv_local, group_blocks, levels + 1),
    )
    live_units = live_units.reshape(units, group_blocks, levels + 1)
    results = lax.map(unit_attend, (query_units, pair_units, live_units))
    results = results.reshape(
        block_groups, kv_local, group_blocks, BLOCK_TOKENS, group_width, HEAD_SIZE
    ).transpose(0, 2, 3, 1, 4, 5)
    return results.reshape(row_count, kv_local * group_width * HEAD_SIZE)


def body(queries, keys, values, pattern, keep):
    kv_pair = jnp.concatenate([keys, values], 1)

    def fetch_earlier(blocks, distance):
        return shifted(blocks, ("seq", "head"), distance)

    return attend(
        queries,
        kv_pair,
        pattern,
        keep,
        fetch_earlier,
        lax.axis_index(("seq", "head")),
        lax.axis_size(("seq", "head")),
    )


def solution(mesh):
    return jax.shard_map(
        body,
        mesh=mesh,
        in_specs=(
            P(("seq", "head"), None),
            P(("seq", "head"), None),
            P(("seq", "head"), None),
            P(),
            P(),
        ),
        out_specs=P(("seq", "head"), None),
        check_vma=False,
    )
```

profile of v0, /device:TPU:191, one launch (start us, length us, event | category | flops | bytes accessed | tf_op | source)
XLA Modules:
  0.0 446.6 jit_solution(1266662776855874604)
XLA Ops:
  2.2 2.8 collective-permute-start
  5.0 3.2 collective-permute-start.1
  8.2 3.9 collective-permute-start.2
  12.1 3.1 collective-permute-start.3
  15.2 3.8 collective-permute-start.4
  21.4 5.4 %copy.60 = bf16[32,8,64,128]{3,2,1,0:T(8,128)(2,1)} copy(bf16[32,8,64,128]{3,1,2,0:T(8,128)(2,1)} %bitcast.148) | data formatting | bytes 8388608
  28.0 8.8 %collective-permute-done = bf16[256,2048]{1,0:T(8,128)(2,1)S(1)} collective-permute-done((bf16[256,2048]{1,0:T(8,128)(2,1)S(1)}, bf16[256,2048]{1,0:T(8,128)(2,1)S(1)}, u32[]{:S(2)}, u32[]{:S(2)}) %collective-permute-start) | collective-permute-done | bytes 1048608 | tf_op jit(solution)/shard_map/ppermute | solution.py:17
  36.8 2.6 collective-permute-start.5
  45.8 1.8 gather_fusion.1
  50.1 22.5 %collective-permute-done.1 = bf16[256,2048]{1,0:T(8,128)(2,1)} collective-permute-done((bf16[256,2048]{1,0:T(8,128)(2,1)S(1)}, bf16[256,2048]{1,0:T(8,128)(2,1)}, u32[]{:S(2)}, u32[]{:S(2)}) %collective-permute-start.1) | collective-permute-done | bytes 1048608 | tf_op jit(solution)/shard_map/ppermute | solution.py:17
  72.6 1.9 collective-permute-start.6
  74.5 1.8 gather_fusion.2
  78.9 16.2 %collective-permute-done.2 = bf16[256,2048]{1,0:T(8,128)(2,1)} collective-permute-done((bf16[256,2048]{1,0:T(8,128)(2,1)S(1)}, bf16[256,2048]{1,0:T(8,128)(2,1)}, u32[]{:S(2)}, u32[]{:S(2)}) %collective-permute-start.2) | collective-permute-done | bytes 1048608 | tf_op jit(solution)/shard_map/ppermute | solution.py:17
  96.5 1.8 gather_fusion.3
  98.4 19.2 %collective-permute-done.3 = bf16[256,2048]{1,0:T(8,128)(2,1)} collective-permute-done((bf16[256,2048]{1,0:T(8,128)(2,1)S(1)}, bf16[256,2048]{1,0:T(8,128)(2,1)}, u32[]{:S(2)}, u32[]{:S(2)}) %collective-permute-start.3) | collective-permute-done | bytes 1048608 | tf_op jit(solution)/shard_map/ppermute | solution.py:17
  117.5 1.8 gather_fusion.4
  127.5 12.5 %collective-permute-done.4 = bf16[256,2048]{1,0:T(8,128)(2,1)} collective-permute-done((bf16[256,2048]{1,0:T(8,128)(2,1)S(1)}, bf16[256,2048]{1,0:T(8,128)(2,1)}, u32[]{:S(2)}, u32[]{:S(2)}) %collective-permute-start.4) | collective-permute-done | bytes 1048608 | tf_op jit(solution)/shard_map/ppermute | solution.py:17
  141.8 44.9 %collective-permute-done.5 = bf16[256,2048]{1,0:T(8,128)(2,1)} collective-permute-done((bf16[256,2048]{1,0:T(8,128)(2,1)S(1)}, bf16[256,2048]{1,0:T(8,128)(2,1)}, u32[]{:S(2)}, u32[]{:S(2)}) %collective-permute-start.5) | collective-permute-done | bytes 1048608 | tf_op jit(solution)/shard_map/ppermute | solution.py:17
  196.8 49.8 %collective-permute-done.6 = bf16[256,2048]{1,0:T(8,128)(2,1)} collective-permute-done((bf16[256,2048]{1,0:T(8,128)(2,1)S(1)}, bf16[256,2048]{1,0:T(8,128)(2,1)}, u32[]{:S(2)}, u32[]{:S(2)}) %collective-permute-start.6) | collective-permute-done | bytes 1048608 | tf_op jit(solution)/shard_map/ppermute | solution.py:17
  246.6 1.8 gather_fusion.7
  248.5 1.8 gather_fusion.8
  251.5 2.4 copy.35
  254.0 2.7 copy.43
  257.9 2.7 copy.44
  260.6 2.6 select_dynamic-update-slice_fusion
  263.3 2.4 constant_dynamic-update-slice_fusion.9
  265.6 2.4 constant_dynamic-update-slice_fusion.8
  268.0 2.4 constant_dynamic-update-slice_fusion.7
  276.4 10.6 %copy.46 = bf16[8,2,2,10,128,128]{5,4,3,2,1,0:T(8,128)(2,1)} copy(bf16[8,2,2,10,128,128]{5,0,1,4,2,3:T(8,128)(2,1)} %bitcast.144) | data formatting | bytes 20971520 | tf_op jit(solution)/shard_map/while | solution.py:96
  287.0 145.7 %while.10 = (s32[]{:T(128)}, bf16[8,2,128,8,128]{2,4,3,1,0:T(8,128)(2,1)}, bf16[8,2,2,10,128,128]{5,4,3,2,1,0:T(8,128)(2,1)}, s32[8,2,10]{2,1,0:T(2,128)S(1)}, b...) while((s32[]{:T(128)}, bf16[8,2,128,8,128]{2,4,3,1,0:T(8,128)(2,1)}, ...), condition=%wide.region_3.5_spmd, body=%wide.region_0.4_spmd.sunk | while | flops 1374236672 | bytes 78194456 | solution.py:96
  288.4 2.7 fusion.24
  291.2 4.0 copy-done.2
  295.1 2.3 fusion.25
  297.5 7.8 %fusion.26 = bf16[8,2,128,8,128]{2,4,3,1,0:T(8,128)(2,1)} fusion(bf16[8,2,128,8,128]{2,4,3,1,0:T(8,128)(2,1)} %get-tuple-element.140, s32[]{:T(128)} %get-tuple-element.139, f32[2,10,128,128,8]{3,2,4,1,0:T(8,128)} %copy-done.2, f32[2,8,128]{2,1,0:T(8,128)S(1)} %fusion.25, f32[2,8,128]{2,1,0:T(8,128)S(1)} %get-tuple-element.130, ...), kind=kOutput, calls=%fused_computation.18.clone.1 | convolution fusion | flops 684457984 | bytes 12010500 | tf_op jit(solution)/shard_map/while/body/eval_jaxpr/grqlp,glpd->gqrd/dot_general | solution.py:39
  306.6 2.7 fusion.24
  309.4 4.0 copy-done.2
  313.4 2.3 fusion.25
  315.7 7.8 %fusion.26 = bf16[8,2,128,8,128]{2,4,3,1,0:T(8,128)(2,1)} fusion(bf16[8,2,128,8,128]{2,4,3,1,0:T(8,128)(2,1)} %get-tuple-element.140, s32[]{:T(128)} %get-tuple-element.139, f32[2,10,128,128,8]{3,2,4,1,0:T(8,128)} %copy-done.2, f32[2,8,128]{2,1,0:T(8,128)S(1)} %fusion.25, f32[2,8,128]{2,1,0:T(8,128)S(1)} %get-tuple-element.130, ...), kind=kOutput, calls=%fused_computation.18.clone.1 | convolution fusion | flops 684457984 | bytes 12010500 | tf_op jit(solution)/shard_map/while/body/eval_jaxpr/grqlp,glpd->gqrd/dot_general | solution.py:39
  324.9 2.7 fusion.24
  327.6 4.0 copy-done.2
  331.6 2.3 fusion.25
  333.9 7.8 %fusion.26 = bf16[8,2,128,8,128]{2,4,3,1,0:T(8,128)(2,1)} fusion(bf16[8,2,128,8,128]{2,4,3,1,0:T(8,128)(2,1)} %get-tuple-element.140, s32[]{:T(128)} %get-tuple-element.139, f32[2,10,128,128,8]{3,2,4,1,0:T(8,128)} %copy-done.2, f32[2,8,128]{2,1,0:T(8,128)S(1)} %fusion.25, f32[2,8,128]{2,1,0:T(8,128)S(1)} %get-tuple-element.130, ...), kind=kOutput, calls=%fused_computation.18.clone.1 | convolution fusion | flops 684457984 | bytes 12010500 | tf_op jit(solution)/shard_map/while/body/eval_jaxpr/grqlp,glpd->gqrd/dot_general | solution.py:39
  343.1 2.7 fusion.24
  345.8 4.0 copy-done.2
  349.8 2.3 fusion.25
  352.1 7.8 %fusion.26 = bf16[8,2,128,8,128]{2,4,3,1,0:T(8,128)(2,1)} fusion(bf16[8,2,128,8,128]{2,4,3,1,0:T(8,128)(2,1)} %get-tuple-element.140, s32[]{:T(128)} %get-tuple-element.139, f32[2,10,128,128,8]{3,2,4,1,0:T(8,128)} %copy-done.2, f32[2,8,128]{2,1,0:T(8,128)S(1)} %fusion.25, f32[2,8,128]{2,1,0:T(8,128)S(1)} %get-tuple-element.130, ...), kind=kOutput, calls=%fused_computation.18.clone.1 | convolution fusion | flops 684457984 | bytes 12010500 | tf_op jit(solution)/shard_map/while/body/eval_jaxpr/grqlp,glpd->gqrd/dot_general | solution.py:39
  361.3 2.7 fusion.24
  364.0 4.0 copy-done.2
  368.0 2.3 fusion.25
  370.3 7.8 %fusion.26 = bf16[8,2,128,8,128]{2,4,3,1,0:T(8,128)(2,1)} fusion(bf16[8,2,128,8,128]{2,4,3,1,0:T(8,128)(2,1)} %get-tuple-element.140, s32[]{:T(128)} %get-tuple-element.139, f32[2,10,128,128,8]{3,2,4,1,0:T(8,128)} %copy-done.2, f32[2,8,128]{2,1,0:T(8,128)S(1)} %fusion.25, f32[2,8,128]{2,1,0:T(8,128)S(1)} %get-tuple-element.130, ...), kind=kOutput, calls=%fused_computation.18.clone.1 | convolution fusion | flops 684457984 | bytes 12010500 | tf_op jit(solution)/shard_map/while/body/eval_jaxpr/grqlp,glpd->gqrd/dot_general | solution.py:39
  379.5 2.7 fusion.24
  382.2 4.0 copy-done.2
  386.2 2.3 fusion.25
  388.5 7.8 %fusion.26 = bf16[8,2,128,8,128]{2,4,3,1,0:T(8,128)(2,1)} fusion(bf16[8,2,128,8,128]{2,4,3,1,0:T(8,128)(2,1)} %get-tuple-element.140, s32[]{:T(128)} %get-tuple-element.139, f32[2,10,128,128,8]{3,2,4,1,0:T(8,128)} %copy-done.2, f32[2,8,128]{2,1,0:T(8,128)S(1)} %fusion.25, f32[2,8,128]{2,1,0:T(8,128)S(1)} %get-tuple-element.130, ...), kind=kOutput, calls=%fused_computation.18.clone.1 | convolution fusion | flops 684457984 | bytes 12010500 | tf_op jit(solution)/shard_map/while/body/eval_jaxpr/grqlp,glpd->gqrd/dot_general | solution.py:39
  397.7 2.7 fusion.24
  400.4 4.0 copy-done.2
  404.4 2.3 fusion.25
  406.7 7.8 %fusion.26 = bf16[8,2,128,8,128]{2,4,3,1,0:T(8,128)(2,1)} fusion(bf16[8,2,128,8,128]{2,4,3,1,0:T(8,128)(2,1)} %get-tuple-element.140, s32[]{:T(128)} %get-tuple-element.139, f32[2,10,128,128,8]{3,2,4,1,0:T(8,128)} %copy-done.2, f32[2,8,128]{2,1,0:T(8,128)S(1)} %fusion.25, f32[2,8,128]{2,1,0:T(8,128)S(1)} %get-tuple-element.130, ...), kind=kOutput, calls=%fused_computation.18.clone.1 | convolution fusion | flops 684457984 | bytes 12010500 | tf_op jit(solution)/shard_map/while/body/eval_jaxpr/grqlp,glpd->gqrd/dot_general | solution.py:39
  415.9 2.7 fusion.24
  418.7 4.0 copy-done.2
  422.7 2.3 fusion.25
  425.0 7.8 %fusion.26 = bf16[8,2,128,8,128]{2,4,3,1,0:T(8,128)(2,1)} fusion(bf16[8,2,128,8,128]{2,4,3,1,0:T(8,128)(2,1)} %get-tuple-element.140, s32[]{:T(128)} %get-tuple-element.139, f32[2,10,128,128,8]{3,2,4,1,0:T(8,128)} %copy-done.2, f32[2,8,128]{2,1,0:T(8,128)S(1)} %fusion.25, f32[2,8,128]{2,1,0:T(8,128)S(1)} %get-tuple-element.130, ...), kind=kOutput, calls=%fused_computation.18.clone.1 | convolution fusion | flops 684457984 | bytes 12010500 | tf_op jit(solution)/shard_map/while/body/eval_jaxpr/grqlp,glpd->gqrd/dot_general | solution.py:39
  432.8 6.6 %copy.48 = bf16[1,2,128,8,8,128]{5,4,3,2,1,0:T(8,128)(2,1)} copy(bf16[1,2,128,8,8,128]{2,5,4,1,3,0:T(8,128)(2,1)} %bitcast.149) | data formatting | bytes 8388608 | tf_op jit(solution)/shard_map/transpose | solution.py:99
  439.3 7.3 %reshape.180 = bf16[256,8192]{1,0:T(8,128)(2,1)} reshape(bf16[1,2,128,8,8,128]{5,4,3,2,1,0:T(8,128)(2,1)} %copy.48) | data formatting | bytes 8388608 | tf_op jit(solution)/shard_map/reshape | solution.py:100
  (114 shorter events, 57.7 us)
Async XLA Ops:
  0.0 20.2 %copy-start = (s32[512,16]{0,1:T(8,128)S(1)}, s32[512,16]{0,1:T(8,128)}, u32[]{:S(2)}) copy-start(s32[512,16]{0,1:T(8,128)} %param.13) | copy-start | bytes 98308
  2.2 34.6 %collective-permute-start = (bf16[256,2048]{1,0:T(8,128)(2,1)S(1)}, bf16[256,2048]{1,0:T(8,128)(2,1)S(1)}, u32[]{:S(2)}, u32[]{:S(2)}) collective-permute-start(bf16[256,2048]{1,0:T(8,128)(2,1)S(1)} %constant_dynamic-update-slice_fusion), channel_id=1, source_target_pairs={{0,1},{1,2},{2,3},{3,4},{4,5},{5,6},{6,7},{7,8},{8,9},{9,10},{10,1... | collective-permute-start | bytes 3145736 | tf_op jit(solution)/shard_map/ppermute | solution.py:17
  5.0 67.6 %collective-permute-start.1 = (bf16[256,2048]{1,0:T(8,128)(2,1)S(1)}, bf16[256,2048]{1,0:T(8,128)(2,1)}, u32[]{:S(2)}, u32[]{:S(2)}) collective-permute-start(bf16[256,2048]{1,0:T(8,128)(2,1)S(1)} %constant_dynamic-update-slice_fusion), channel_id=1, source_target_pairs={{0,2},{1,3},{2,4},{3,5},{4,6},{5,7},{6,8},{7,9},{8,10},{9,11},{10,... | collective-permute-start | bytes 3145736 | tf_op jit(solution)/shard_map/ppermute | solution.py:17
  8.2 86.9 %collective-permute-start.2 = (bf16[256,2048]{1,0:T(8,128)(2,1)S(1)}, bf16[256,2048]{1,0:T(8,128)(2,1)}, u32[]{:S(2)}, u32[]{:S(2)}) collective-permute-start(bf16[256,2048]{1,0:T(8,128)(2,1)S(1)} %constant_dynamic-update-slice_fusion), channel_id=1, source_target_pairs={{0,4},{1,5},{2,6},{3,7},{4,8},{5,9},{6,10},{7,11},{8,12},{9,13},{1... | collective-permute-start | bytes 3145736 | tf_op jit(solution)/shard_map/ppermute | solution.py:17
  12.1 105.4 %collective-permute-start.3 = (bf16[256,2048]{1,0:T(8,128)(2,1)S(1)}, bf16[256,2048]{1,0:T(8,128)(2,1)}, u32[]{:S(2)}, u32[]{:S(2)}) collective-permute-start(bf16[256,2048]{1,0:T(8,128)(2,1)S(1)} %constant_dynamic-update-slice_fusion), channel_id=1, source_target_pairs={{0,8},{1,9},{2,10},{3,11},{4,12},{5,13},{6,14},{7,15},{8,16},{9,17... | collective-permute-start | bytes 3145736 | tf_op jit(solution)/shard_map/ppermute | solution.py:17
  15.2 124.7 %collective-permute-start.4 = (bf16[256,2048]{1,0:T(8,128)(2,1)S(1)}, bf16[256,2048]{1,0:T(8,128)(2,1)}, u32[]{:S(2)}, u32[]{:S(2)}) collective-permute-start(bf16[256,2048]{1,0:T(8,128)(2,1)S(1)} %constant_dynamic-update-slice_fusion), channel_id=1, source_target_pairs={{0,16},{1,17},{2,18},{3,19},{4,20},{5,21},{6,22},{7,23},{8,24},{9,... | collective-permute-start | bytes 3145736 | tf_op jit(solution)/shard_map/ppermute | solution.py:17
  36.8 2.6 copy-start.8
  36.8 149.9 %collective-permute-start.5 = (bf16[256,2048]{1,0:T(8,128)(2,1)S(1)}, bf16[256,2048]{1,0:T(8,128)(2,1)}, u32[]{:S(2)}, u32[]{:S(2)}) collective-permute-start(bf16[256,2048]{1,0:T(8,128)(2,1)S(1)} %constant_dynamic-update-slice_fusion), channel_id=1, source_target_pairs={{0,32},{1,33},{2,34},{3,35},{4,36},{5,37},{6,38},{7,39},{8,40},{9,... | collective-permute-start | bytes 3145736 | tf_op jit(solution)/shard_map/ppermute | solution.py:17
  72.6 174.0 %collective-permute-start.6 = (bf16[256,2048]{1,0:T(8,128)(2,1)S(1)}, bf16[256,2048]{1,0:T(8,128)(2,1)}, u32[]{:S(2)}, u32[]{:S(2)}) collective-permute-start(bf16[256,2048]{1,0:T(8,128)(2,1)S(1)} %constant_dynamic-update-slice_fusion), channel_id=1, source_target_pairs={{0,64},{1,65},{2,66},{3,67},{4,68},{5,69},{6,70},{7,71},{8,72},{9,... | collective-permute-start | bytes 3145736 | tf_op jit(solution)/shard_map/ppermute | solution.py:17
  95.0 153.4 %collective-permute-start.7 = (bf16[256,2048]{1,0:T(8,128)(2,1)S(1)}, bf16[256,2048]{1,0:T(8,128)(2,1)}, u32[]{:S(2)}, u32[]{:S(2)}) collective-permute-start(bf16[256,2048]{1,0:T(8,128)(2,1)S(1)} %constant_dynamic-update-slice_fusion), channel_id=1, source_target_pairs={{0,128},{1,129},{2,130},{3,131},{4,132},{5,133},{6,134},{7,135},{8... | collective-permute-start | bytes 3145736 | tf_op jit(solution)/shard_map/ppermute | solution.py:17
  251.5 18.9 %copy-start.3 = (bf16[1,2,1,128,2,8,128]{6,5,4,3,1,2,0:T(8,128)(2,1)S(1)}, bf16[1,2,1,128,2,8,128]{6,5,4,3,1,2,0:T(8,128)(2,1)}, u32[]{:S(2)}) copy-start(bf16[1,2,1,128,2,8,128]{6,5,4,3,1,2,0:T(8,128)(2,1)} %copy.40) | copy-start | bytes 3145732
  251.5 20.1 %copy-start.4 = (bf16[1,2,1,128,2,8,128]{6,5,4,3,1,2,0:T(8,128)(2,1)S(1)}, bf16[1,2,1,128,2,8,128]{6,5,4,3,1,2,0:T(8,128)(2,1)}, u32[]{:S(2)}) copy-start(bf16[1,2,1,128,2,8,128]{6,5,4,3,1,2,0:T(8,128)(2,1)} %copy.41) | copy-start | bytes 3145732
  257.9 14.9 %copy-start.5 = (bf16[1,2,1,128,2,8,128]{6,5,4,3,1,2,0:T(8,128)(2,1)S(1)}, bf16[1,2,1,128,2,8,128]{6,5,4,3,1,2,0:T(8,128)(2,1)}, u32[]{:S(2)}) copy-start(bf16[1,2,1,128,2,8,128]{6,5,4,3,1,2,0:T(8,128)(2,1)} %copy.42) | copy-start | bytes 3145732
  260.6 13.4 %copy-start.6 = (bf16[1,2,1,128,2,8,128]{6,5,4,3,1,2,0:T(8,128)(2,1)S(1)}, bf16[1,2,1,128,2,8,128]{6,5,4,3,1,2,0:T(8,128)(2,1)}, u32[]{:S(2)}) copy-start(bf16[1,2,1,128,2,8,128]{6,5,4,3,1,2,0:T(8,128)(2,1)} %copy.43) | copy-start | bytes 3145732
  260.6 14.6 %copy-start.7 = (bf16[1,2,1,128,2,8,128]{6,5,4,3,1,2,0:T(8,128)(2,1)S(1)}, bf16[1,2,1,128,2,8,128]{6,5,4,3,1,2,0:T(8,128)(2,1)}, u32[]{:S(2)}) copy-start(bf16[1,2,1,128,2,8,128]{6,5,4,3,1,2,0:T(8,128)(2,1)} %copy.44) | copy-start | bytes 3145732
  291.1 4.0 copy-start.2
  309.4 4.0 copy-start.2
  327.6 4.0 copy-start.2
  345.8 4.0 copy-start.2
  364.0 4.0 copy-start.2
  382.2 4.0 copy-start.2
  400.4 4.0 copy-start.2
  418.7 4.0 copy-start.2
  432.8 13.8 %copy-start.1 = (s32[512,16]{0,1:T(8,128)S(1)}, s32[512,16]{0,1:T(8,128)}, u32[]{:S(2)}) copy-start(s32[512,16]{0,1:T(8,128)} %param.13) | copy-start | bytes 98308
where the time goes:
time: 449 us; the launch traced here: 447 us
  waiting for transfers between devices  174 us (39%)
  local copies, waits for them, and re-layouts  134 us (30%)
  matrix products  84.3 us (19%)
  other arithmetic  31.1 us (7%)
  starting transfers between devices  22.8 us (5%)
    ppermute x8, waiting for transfers between devices, shifted(): return lax.ppermute(x, axis, pairs)  174 us
    dot_general x8, matrix products, unit_attend(): jnp.einsum('grqlp,glpd->gqrd', weights, pair_unit[1], preferred_element_t...  62.5 us
    while x16, local copies, waits for them, and re-layouts  31.9 us
    ppermute x8, starting transfers between devices, shifted(): return lax.ppermute(x, axis, pairs)  22.8 us
    dot_general x8, matrix products, unit_attend(): jnp.einsum('gqrd,glpd->grqlp', query_unit, pair_unit[0], preferred_elemen...  21.8 us
    unnamed x28, local copies, waits for them, and re-layouts  19.9 us
    gather x11, local copies, waits for them, and re-layouts, attend(): chosen.append(jnp.take(source, local_index, axis=0))  19.6 us
    reduce_sum x8, other arithmetic, unit_attend(): jnp.sum(expo, axis=(3, 4), keepdims=True)  18.5 us
  transfers between devices with their start and end apart: 8, of which 7 were waited for; matrix products, arithmetic and copies ran while one was open for 11% of the time, Pallas kernels for 0%

commit v1 on v0

v1 whole, which is shorter than its diff:
```python
import functools
import math

import jax
import jax.numpy as jnp
from jax import lax
from jax.experimental import pallas as pl
from jax.experimental.pallas import tpu as pltpu
from jax.sharding import PartitionSpec as P

GROUP = 8
KV_HEADS = 8
HEAD = 128
BLOCK = 128
LEVELS = 9
UNITS = 2 * KV_HEADS
SCALE = 1.0 / math.sqrt(HEAD)
NEG = -1e30
MESH = pl.DeviceIdType.MESH

R1, R2, R4, R8, R16, R32, R64, R128, VIA = range(9)
PIECES = 4


def piece_of(pair, piece):
    return pair[piece // 2].at[pl.ds((piece % 2) * BLOCK, BLOCK)]


def kernel(comm, q_hbm, k_hbm, v_hbm, pattern_hbm, keep_hbm, out_hbm, *scratch):
    buffers = scratch[:20]
    (q, out, acc, peak, pattern, keep, choice, blind, load_sem, out_sem, send_sem, recv_sem) = scratch[20:]
    own_hbm = (k_hbm, v_hbm)
    own = (buffers[0], buffers[1])
    slots = [(buffers[2 + 2 * i], buffers[3 + 2 * i]) for i in range(9)]

    if comm:
        s, h = lax.axis_index("seq"), lax.axis_index("head")
    else:
        s, h = jnp.int32(17), jnp.int32(3)
    z, x, y, c = s // 4, s % 4, h // 2, h % 2
    me = s * 8 + h

    def at(dz=0, dx=0, dy=0, dc=0):
        return (
            ((z + dz + 8) % 8) * 4 + (x + dx + 4) % 4,
            ((y + dy + 4) % 4) * 2 + (c + dc) % 2,
        )

    row0 = (me // 4) * 8
    loads = [
        pltpu.make_async_copy(pattern_hbm.at[pl.ds(row0, 8)], pattern, load_sem.at[0]),
        pltpu.make_async_copy(keep_hbm.at[pl.ds(row0, 8)], keep, load_sem.at[1]),
        pltpu.make_async_copy(k_hbm, own[0], load_sem.at[2]),
        pltpu.make_async_copy(v_hbm, own[1], load_sem.at[3]),
        pltpu.make_async_copy(q_hbm, q, load_sem.at[4]),
    ]
    for load in loads:
        load.start()

    def remote(source, slot, piece, lane, target):
        return pltpu.make_async_remote_copy(
            src_ref=piece_of(source, piece),
            dst_ref=piece_of(slots[slot], piece),
            send_sem=send_sem.at[lane, piece],
            recv_sem=recv_sem.at[slot, piece],
            device_id=target,
            device_id_type=MESH,
        )

    def arrived(slot, piece):
        if comm:
            remote(slots[slot], slot, piece, 0, at(dz=1)).wait_recv()

    Z1, X1, Y1, C1, Z2, X2, X2B, Y2, Y2B, ZP, ZM, ZM2 = range(12)

    def send(source, slot, piece, lane, target):
        remote(source, slot, piece, lane, target).start()

    if comm:
        barrier = pltpu.get_barrier_semaphore()
        partners = [
            at(dz=1), at(dz=-1), at(dz=2), at(dz=-2), at(dx=1), at(dx=-1), at(dx=2),
            at(dy=1), at(dy=-1), at(dy=2), at(dc=1),
        ]
        for partner in partners:
            pl.semaphore_signal(barrier, inc=1, device_id=partner, device_id_type=MESH)
        pl.semaphore_wait(barrier, len(partners))

        for piece in range(PIECES):
            send(own_hbm, R32, piece, Z1, at(dz=1))

            @pl.when(x < 3)
            def _():
                send(own_hbm, R8, piece, X1, at(dx=1))

            @pl.when(y < 3)
            def _():
                send(own_hbm, R2, piece, Y1, at(dy=1))

            @pl.when(c == 0)
            def _():
                send(own_hbm, R1, piece, C1, at(dc=1))

            if piece >= 2:
                send(own_hbm, VIA, piece, ZM, at(dz=-2))

    for load in loads:
        load.wait()

    line = lax.broadcasted_iota(jnp.int32, pattern.shape, 0)
    column = lax.broadcasted_iota(jnp.int32, pattern.shape, 1)
    blocks, kept = pattern[...].astype(jnp.float32), keep[...].astype(jnp.float32)
    for j in range(2):
        for level in range(LEVELS):
            here = (line == (me % 4) * 2 + j) & (column == level)

            def entry(table):
                found = jnp.where(here, table, 0.0)
                return jnp.sum(jnp.sum(found, axis=1, keepdims=True), axis=0, keepdims=True)

            if level >= 1:
                base = (2 * (me - 2 ** (level - 1))).astype(jnp.float32)
                block = jnp.clip(entry(blocks) - base, 0.0, 1.0)
                choice[j * LEVELS + level] = jnp.broadcast_to(block, (BLOCK, HEAD)).astype(jnp.bfloat16)
            blind[j * LEVELS + level] = jnp.broadcast_to((entry(kept) - 1.0) * -NEG, (8, HEAD))

    def attend(j_g, sources, first=False, last=False):
        j, g = j_g
        unit = j * KV_HEADS + g
        rows = pl.ds(pl.multiple_of(j * BLOCK, BLOCK), BLOCK)
        kv_columns = pl.ds(pl.multiple_of(g * HEAD, HEAD), HEAD)
        ones = jnp.ones((BLOCK, HEAD), jnp.bfloat16)
        keys, values, biases = [], [], []
        for pair, block, level in sources:
            table = j * LEVELS + level

            def taken(ref):
                if block is not None:
                    start = block * BLOCK
                    if not isinstance(block, int):
                        start = pl.multiple_of(start, BLOCK)
                    return ref[pl.ds(start, BLOCK), kv_columns]
                first_block, second_block = (
                    ref[pl.ds(i * BLOCK, BLOCK), kv_columns] for i in range(2)
                )
                second = choice[table]
                return first_block * (1 - second) + second_block * second

            keys.append(taken(pair[0]))
            values.append(jnp.concatenate([taken(pair[1]), ones], 1))
            biases.append(blind[table][:1])
        keys = jnp.concatenate(keys, 0)
        values = jnp.concatenate(values, 0)
        queries = jnp.concatenate(
            [
                q[rows, pl.ds(pl.multiple_of((g * GROUP + r) * HEAD, HEAD), HEAD)]
                for r in range(GROUP)
            ],
            0,
        )
        scores = lax.dot_general(
            queries, keys, (((1,), (1,)), ((), ())), preferred_element_type=jnp.float32
        )
        parts = []
        for i, bias in enumerate(biases):
            part = scores[:, i * BLOCK : (i + 1) * BLOCK]
            if first:
                token = lax.broadcasted_iota(jnp.int32, part.shape, 0) % BLOCK
                key = lax.broadcasted_iota(jnp.int32, part.shape, 1)
                part = jnp.where(key <= token, part, NEG)
            else:
                part = part + bias
            parts.append(part)
        top = functools.reduce(jnp.maximum, parts)
        top = jnp.max(top, axis=1, keepdims=True)
        top = jnp.broadcast_to(top, (GROUP * BLOCK, HEAD))
        if not first:
            before = peak[unit]
            top = jnp.maximum(before, top)
        weights = [jnp.exp((part - top) * SCALE).astype(jnp.bfloat16) for part in parts]
        weights = jnp.concatenate(weights, 1) if len(weights) > 1 else weights[0]
        total = jnp.dot(weights, values, preferred_element_type=jnp.float32)
        if not first:
            fade = jnp.exp((before - top) * SCALE)
            total = total + acc[unit] * jnp.concatenate([fade, fade], 1)
        if last:
            result = (total[:, :HEAD] / total[:, HEAD:]).astype(jnp.bfloat16)
            for r in range(GROUP):
                columns = pl.ds(pl.multiple_of((g * GROUP + r) * HEAD, HEAD), HEAD)
                out[rows, columns] = result[r * BLOCK : (r + 1) * BLOCK]
        else:
            acc[unit] = total
            peak[unit] = top

    def sweep(sources_of, first=False, last=False):
        def step(unit, carry):
            j, g = unit // KV_HEADS, unit % KV_HEADS
            attend((j, g), sources_of(j), first, last)
            if last:
                columns = pl.ds(pl.multiple_of(g * GROUP * HEAD, HEAD), GROUP * HEAD)
                rows = pl.ds(pl.multiple_of(j * BLOCK, BLOCK), BLOCK)
                pltpu.make_async_copy(
                    out.at[rows, columns], out_hbm.at[rows, columns], out_sem.at[unit]
                ).start()
            return carry

        lax.fori_loop(0, UNITS, step, 0)

    def level_source(level, slot):
        return lambda j: (slots[slot], None, level)

    sweep(lambda j: [(own, j, 0)], first=True)

    for piece in range(PIECES):
        arrived(R32, piece)
        if comm:
            send(slots[R32], R64, piece, Z2, at(dz=1))

            @pl.when(x == 3)
            def _():
                send(slots[R32], R8, piece, X1, at(dx=1))

            @pl.when(x == 2)
            def _():
                send(slots[R32], R16, piece, X2B, at(dx=2))

        arrived(R8, piece)
        if comm:

            @pl.when(x < 3)
            def _():
                send(slots[R8], R16, piece, X2, at(dx=1))

            @pl.when(y == 3)
            def _():
                send(slots[R8], R2, piece, Y1, at(dy=1))

            @pl.when(y == 2)
            def _():
                send(slots[R8], R4, piece, Y2B, at(dy=2))

        arrived(R2, piece)
        if comm:

            @pl.when(y < 3)
            def _():
                send(slots[R2], R4, piece, Y2, at(dy=1))

            @pl.when(c == 1)
            def _():
                send(slots[R2], R1, piece, C1, at(dc=1))

    for piece in (2, 3):
        arrived(VIA, piece)
        if comm:
            send(slots[VIA], R128, piece, ZM2, at(dz=-2))

    level2, level4 = level_source(2, R2), level_source(4, R8)
    level6, level3 = level_source(6, R32), level_source(3, R4)
    level5, level7 = level_source(5, R16), level_source(7, R64)
    level8 = level_source(8, R128)
    sweep(lambda j: [level6(j), level4(j)])

    for piece in (0, 1):
        arrived(R64, piece)
        if comm:
            send(slots[R64], R128, piece, ZP, at(dz=2))

    for piece in range(PIECES):
        arrived(R1, piece)
    level1 = level_source(1, R1)

    def near_sweep(j):
        def step(g, carry):
            source = (slots[R1], 1, 0) if j == 0 else (own, 0, 0)
            attend((j, g), [source, level1(j), level2(j)])
            return carry

        lax.fori_loop(0, KV_HEADS, step, 0)

    near_sweep(0)
    near_sweep(1)

    for piece in (2, 3):
        arrived(R64, piece)
    for piece in range(PIECES):
        arrived(R16, piece)
        arrived(R4, piece)
    sweep(lambda j: [level7(j), level5(j), level3(j)])

    for piece in range(PIECES):
        arrived(R128, piece)
    sweep(lambda j: [level8(j)], last=True)

    def drain(unit, carry):
        j, g = unit // KV_HEADS, unit % KV_HEADS
        columns = pl.ds(pl.multiple_of(g * GROUP * HEAD, HEAD), GROUP * HEAD)
        rows = pl.ds(pl.multiple_of(j * BLOCK, BLOCK), BLOCK)
        pltpu.make_async_copy(
            out.at[rows, columns], out_hbm.at[rows, columns], out_sem.at[unit]
        ).wait()
        return carry

    lax.fori_loop(0, UNITS, drain, 0)

    if comm:

        def sent(lane, piece):
            remote(own, R1, piece, lane, at(dz=1)).wait_send()

        for piece in range(PIECES):
            for lane in (Z1, X1, Y1, C1, Z2):
                sent(lane, piece)

            @pl.when(x < 3)
            def _():
                sent(X2, piece)

            @pl.when(x == 2)
            def _():
                sent(X2B, piece)

            @pl.when(y < 3)
            def _():
                sent(Y2, piece)

            @pl.when(y == 2)
            def _():
                sent(Y2B, piece)

            if piece < 2:
                sent(ZP, piece)
            else:
                sent(ZM, piece)
                sent(ZM2, piece)


def body(queries, keys, values, pattern, keep, comm=True):
    rows, width = queries.shape
    kv = pltpu.VMEM(keys.shape, keys.dtype)
    return pl.pallas_call(
        functools.partial(kernel, comm),
        out_shape=jax.ShapeDtypeStruct((rows, width), queries.dtype),
        in_specs=[pl.BlockSpec(memory_space=pl.ANY)] * 5,
        out_specs=pl.BlockSpec(memory_space=pl.ANY),
        scratch_shapes=[kv] * 20
        + [
            pltpu.VMEM((rows, width), queries.dtype),
            pltpu.VMEM((rows, width), queries.dtype),
            pltpu.VMEM((UNITS, GROUP * BLOCK, 2 * HEAD), jnp.float32),
            pltpu.VMEM((UNITS, GROUP * BLOCK, HEAD), jnp.float32),
            pltpu.VMEM((8, pattern.shape[1]), jnp.int32),
            pltpu.VMEM((8, keep.shape[1]), jnp.int32),
            pltpu.VMEM((2 * LEVELS, BLOCK, HEAD), jnp.bfloat16),
            pltpu.VMEM((2 * LEVELS, 8, HEAD), jnp.float32),
            pltpu.SemaphoreType.DMA((5,)),
            pltpu.SemaphoreType.DMA((UNITS,)),
            pltpu.SemaphoreType.DMA((12, PIECES)),
            pltpu.SemaphoreType.DMA((9, PIECES)),
        ],
        compiler_params=pltpu.CompilerParams(
            vmem_limit_bytes=63 * 1024 * 1024,
            **(dict(collective_id=0, has_side_effects=True) if comm else {}),
        ),
        name="butterfly_attention",
    )(queries, keys, values, pattern, keep)


def solution(mesh):
    return jax.shard_map(
        body,
        mesh=mesh,
        in_specs=(
            P(("seq", "head"), None),
            P(("seq", "head"), None),
            P(("seq", "head"), None),
            P(),
            P(),
        ),
        out_specs=P(("seq", "head"), None),
        check_vma=False,
    )
```

time: 449 us -> 138 us (0.31)
  the two profiles are of different devices: /device:TPU:191 before, /device:TPU:32 now
where the time goes in v1:
time: 138 us
  Pallas kernels  130 us (94%)
  local copies, waits for them, and re-layouts  7.81 us (6%)
    pallas_call x1, Pallas kernels, body(): pl.pallas_call(functools.partial(kernel, comm), out_shape=jax.ShapeDtypeS...  130 us
    unnamed x3, local copies, waits for them, and re-layouts  7.81 us

profile of v1, /device:TPU:32, one launch (start us, length us, event | category | flops | bytes accessed | tf_op | source)
XLA Modules:
  0.0 138.2 jit_solution(702892368944863810)
XLA Ops:
  0.0 1.6 %copy.6.pattern_hbm = s32[512,16]{1,0:T(8,128)} copy(s32[512,16]{0,1:T(8,128)} %param.8) | data formatting | bytes 65536 | tf_op args[3]
  1.6 1.6 %copy.7.keep_hbm = s32[512,16]{1,0:T(8,128)} copy(s32[512,16]{0,1:T(8,128)} %param.9) | data formatting | bytes 65536 | tf_op args[4]
  3.2 130.4 %butterfly_attention.1 = bf16[256,8192]{1,0:T(8,128)(2,1)} custom-call(bf16[256,8192]{1,0:T(8,128)(2,1)} %q_hbm.1, bf16[256,1024]{1,0:T(8,128)(2,1)} %k_hbm.1, bf16[256,1024]{1,0:T(8,128)(2,1)} %v_hbm.1, s32[512,16]{1,0:T(8,128)} %copy.6.pattern_hbm, s32[512,16]{1,0:T(8,128)} %copy.7.keep_hbm), custom_call_target="tpu_custom_call" | custom-call | tf_op jit(solution)/shard_map/butterfly_attention/pallas_call | solution.py:341
  133.5 4.6 %copy.9 = bf16[256,8192]{1,0:T(8,128)(2,1)} copy(bf16[256,8192]{1,0:T(8,128)(2,1)} %butterfly_attention.1) | data formatting | bytes 8388608

commit v2 on v1

v2 whole, which is shorter than its diff:
```python
import functools
import math

import jax
import jax.numpy as jnp
from jax import lax
from jax.experimental import pallas as pl
from jax.experimental.pallas import tpu as pltpu
from jax.sharding import PartitionSpec as P

GROUP = 8
KV_HEADS = 8
HEAD = 128
BLOCK = 128
LEVELS = 9
STEEP = math.log2(math.e) / math.sqrt(HEAD)
TILE = 8
WIDE = 2
NEG = -1e30
MESH = pl.DeviceIdType.MESH

R1, R2, R4, R8, R16, R32, R64, R128, VIA_Z, VIA_X, VIA_Y = range(11)
SLOTS = 11
PIECES = 4
HALF = KV_HEADS // 2


def piece_of(pair, which, half, rows=(0, 2 * BLOCK)):
    columns = pl.ds(pl.multiple_of(half * HALF * HEAD, HALF * HEAD), HALF * HEAD)
    return pair[which].at[pl.ds(rows[0], rows[1]), columns]


UPPER, LOWER = (0, BLOCK), (BLOCK, BLOCK)


def kernel(comm, q_hbm, k_hbm, v_hbm, pattern_hbm, keep_hbm, out_hbm, *scratch):
    buffers = scratch[: 2 * SLOTS + 2]
    (q, q_rest, out, acc, mass, peak, pattern, keep, choice, blind, load_sem, out_sem, send_sem, recv_sem) = scratch[2 * SLOTS + 2 :]
    own_hbm = (k_hbm, v_hbm)
    own = (buffers[0], buffers[1])
    slots = [(buffers[2 + 2 * i], buffers[3 + 2 * i]) for i in range(SLOTS)]

    if comm:
        s, h = lax.axis_index("seq"), lax.axis_index("head")
    else:
        s, h = jnp.int32(17), jnp.int32(3)
    z, x, y, c = s // 4, s % 4, h // 2, h % 2
    me = s * 8 + h

    def at(dz=0, dx=0, dy=0, dc=0):
        return (
            ((z + dz + 8) % 8) * 4 + (x + dx + 4) % 4,
            ((y + dy + 4) % 4) * 2 + (c + dc) % 2,
        )

    lanes = pl.ds(pl.multiple_of((me // 64) * HEAD, HEAD), HEAD)
    loads = [
        pltpu.make_async_copy(pattern_hbm.at[:, lanes], pattern, load_sem.at[0]),
        pltpu.make_async_copy(keep_hbm.at[:, lanes], keep, load_sem.at[1]),
        pltpu.make_async_copy(k_hbm, own[0], load_sem.at[2]),
        pltpu.make_async_copy(v_hbm, own[1], load_sem.at[3]),
        pltpu.make_async_copy(q_hbm, q, load_sem.at[4]),
    ]
    for load in loads:
        load.start()

    def remote(source, slot, which, half, lane, target, rows=(0, 2 * BLOCK), sem=None):
        piece = 2 * half + which if sem is None else sem
        return pltpu.make_async_remote_copy(
            src_ref=piece_of(source, which, half, rows),
            dst_ref=piece_of(slots[slot], which, half, rows),
            send_sem=send_sem.at[lane, piece],
            recv_sem=recv_sem.at[slot, piece],
            device_id=target,
            device_id_type=MESH,
        )

    def arrived(slot, which, half, rows=(0, 2 * BLOCK), sem=None):
        if comm:
            remote(slots[slot], slot, which, half, 0, at(dz=1), rows, sem).wait_recv()

    Z1, X1, Y1, C1, Z2, X2, XB, XB2, Y2, YB, YB2, ZP, ZM, ZM2 = range(14)

    def send(*args, **kwargs):
        if comm:
            remote(*args, **kwargs).start()

    def where(condition, do):
        if comm:
            pl.when(condition)(do)

    if comm:
        barrier = pltpu.get_barrier_semaphore()
        partners = [
            at(dz=1), at(dz=-1), at(dz=2), at(dz=-2), at(dx=1), at(dx=-1), at(dy=1), at(dy=-1), at(dc=1),
        ]
        for partner in partners:
            pl.semaphore_signal(barrier, inc=1, device_id=partner, device_id_type=MESH)
        pl.semaphore_wait(barrier, len(partners))

        for half in range(2):
            for which in range(2):
                send(own_hbm, R32, which, half, Z1, at(dz=1))
                where(x < 3, lambda: send(own_hbm, R8, which, half, X1, at(dx=1)))
                where(y < 3, lambda: send(own_hbm, R2, which, half, Y1, at(dy=1)))
                where(c == 0, lambda: send(own_hbm, R1, which, half, C1, at(dc=1)))
                if which == 1:
                    send(own_hbm, VIA_Z, 1, half, ZM, at(dz=-2))
        send(own_hbm, VIA_Z, 0, 1, ZM, at(dz=-2), LOWER)

    for load in loads:
        load.wait()

    line = lax.broadcasted_iota(jnp.int32, pattern.shape, 0)
    column = lax.broadcasted_iota(jnp.int32, pattern.shape, 1)
    blocks, kept = pattern[...].astype(jnp.float32), keep[...].astype(jnp.float32)
    for j in range(2):
        for level in range(LEVELS):
            here = (line == level) & (column == (me % 64) * 2 + j)

            def entry(table):
                found = jnp.where(here, table, 0.0)
                return jnp.sum(jnp.sum(found, axis=1, keepdims=True), axis=0, keepdims=True)

            if level >= 1:
                base = (2 * (me - 2 ** (level - 1))).astype(jnp.float32)
                block = jnp.clip(entry(blocks) - base, 0.0, 1.0)
                choice[j * LEVELS + level] = jnp.broadcast_to(block, (BLOCK, HEAD)).astype(jnp.bfloat16)
            blind[j * LEVELS + level] = jnp.broadcast_to((entry(kept) - 1.0) * -NEG, (8, HEAD))

    def queries_of(item, first):
        j, g, t = item
        rows = pl.ds(j * BLOCK, BLOCK)
        found = []
        for r in range(TILE):
            columns = pl.ds(pl.multiple_of((g * GROUP + t * TILE + r) * HEAD, HEAD), HEAD)
            if first:
                scaled = q[rows, columns].astype(jnp.float32) * STEEP
                whole = scaled.astype(jnp.bfloat16)
                rest = (scaled - whole.astype(jnp.float32)).astype(jnp.bfloat16)
                q[rows, columns], q_rest[rows, columns] = whole, rest
            else:
                whole, rest = q[rows, columns], q_rest[rows, columns]
            found.append(jnp.concatenate([whole, rest], 1))
        return jnp.concatenate(found, 0) if TILE > 1 else found[0]

    def gathered(j, g, sources):
        columns = pl.ds(pl.multiple_of(g * HEAD, HEAD), HEAD)

        def taken(ref, block, level):
            if block is not None:
                return ref[pl.ds(block * BLOCK, BLOCK), columns]
            first_block, second_block = (ref[pl.ds(i * BLOCK, BLOCK), columns] for i in range(2))
            second = choice[j * LEVELS + level]
            return first_block * (1 - second) + second_block * second

        keys, values = (
            [taken(pair[i], block, level) for pair, block, level in sources] for i in range(2)
        )
        keys = jnp.concatenate(keys, 0) if len(keys) > 1 else keys[0]
        values = jnp.concatenate(values, 0) if len(values) > 1 else values[0]
        return jnp.concatenate([keys, keys], 1), values

    def scores_of(item, keys, first):
        return lax.dot_general(
            queries_of(item, first), keys, (((1,), (1,)), ((), ())),
            preferred_element_type=jnp.float32,
        )

    def finish(item, scores, values, levels, first, last):
        j, g, t = item
        unit = g * 2 + j
        tile = pl.ds(t * TILE * BLOCK, TILE * BLOCK)
        parts = []
        for i, level in enumerate(levels):
            part = scores[:, i * BLOCK : (i + 1) * BLOCK]
            if first:
                token = lax.broadcasted_iota(jnp.int32, part.shape, 0) % BLOCK
                key = lax.broadcasted_iota(jnp.int32, part.shape, 1)
                part = jnp.where(key <= token, part, NEG)
            else:
                part = part + blind[j * LEVELS + level][:1]
            parts.append(part)
        top = functools.reduce(jnp.maximum, parts)
        top = jnp.max(top, axis=1, keepdims=True)
        top = jnp.broadcast_to(top, (TILE * BLOCK, HEAD))
        if not first:
            before = peak[unit, tile]
            top = jnp.maximum(before, top)
        weights = [jnp.exp2(part - top) for part in parts]
        added = functools.reduce(jnp.add, weights)
        weights = [weight.astype(jnp.bfloat16) for weight in weights]
        weights = jnp.concatenate(weights, 1) if len(weights) > 1 else weights[0]
        total = jnp.dot(weights, values, preferred_element_type=jnp.float32)
        if not first:
            fade = jnp.exp2(before - top)
            total = total + acc[unit, tile] * fade
            added = added + mass[unit, tile] * fade
        if last:
            result = (total / jnp.sum(added, axis=1, keepdims=True)).astype(jnp.bfloat16)
            for r in range(TILE):
                columns = pl.ds(pl.multiple_of((g * GROUP + t * TILE + r) * HEAD, HEAD), HEAD)
                out[pl.ds(j * BLOCK, BLOCK), columns] = result[r * BLOCK : (r + 1) * BLOCK]
        else:
            acc[unit, tile] = total
            mass[unit, tile] = added
            peak[unit, tile] = top

    def out_copy(g):
        columns = pl.ds(pl.multiple_of(g * GROUP * HEAD, HEAD), GROUP * HEAD)
        return pltpu.make_async_copy(out.at[:, columns], out_hbm.at[:, columns], out_sem.at[g])

    def sweep(half, sources_of, first=False, last=False):
        def step(i, carry):
            waiting = None
            for g in range(WIDE):
                g = half * HALF + i * WIDE + g
                for j in range(2):
                    sources = sources_of(j)
                    keys, values = gathered(j, g, sources)
                    levels = [level for _, _, level in sources]
                    for t in range(GROUP // TILE):
                        item = (j, g, t)
                        scores = scores_of(item, keys, first)
                        if waiting is not None:
                            finish(*waiting, first, last)
                        waiting = (item, scores, values, levels)
            finish(*waiting, first, last)
            if last:
                for g in range(WIDE):
                    out_copy(half * HALF + i * WIDE + g).start()
            return carry

        lax.fori_loop(0, HALF // WIDE, step, 0)

    def level_source(level, slot):
        return lambda j: (slots[slot], None, level)

    level1, level2 = level_source(1, R1), level_source(2, R2)
    level3, level4 = level_source(3, R4), level_source(4, R8)
    level5, level6 = level_source(5, R16), level_source(6, R32)
    level7, level8 = level_source(7, R64), level_source(8, R128)

    def level0(j):
        return (slots[R1], 1, 0) if j == 0 else (own, 0, 0)

    def halves(phase):
        def step(half, carry):
            phase(half)
            return carry

        lax.fori_loop(0, 2, step, 0)

    halves(lambda half: sweep(half, lambda j: [(own, j, 0)], first=True))

    def phase1(half):
        for which in range(2):
            arrived(R32, which, half)
            send(slots[R32], R64, which, half, Z2, at(dz=1))
            where(x == 3, lambda: send(slots[R32], R8, which, half, X1, at(dx=1)))
            where(x == 2, lambda: send(slots[R32], VIA_X, which, half, XB, at(dx=-1)))
            arrived(R8, which, half)
            where(x < 3, lambda: send(slots[R8], R16, which, half, X2, at(dx=1)))
            where(y == 3, lambda: send(slots[R8], R2, which, half, Y1, at(dy=1)))
            where(y == 2, lambda: send(slots[R8], VIA_Y, which, half, YB, at(dy=-1)))
        arrived(VIA_Z, 1, half)
        send(slots[VIA_Z], R128, 1, half, ZM2, at(dz=-2))
        sweep(half, lambda j: [level6(j), level4(j)])
        for which in range(2):

            def pass_x():
                arrived(VIA_X, which, half)
                send(slots[VIA_X], R16, which, half, XB2, at(dx=-1))

            where(x == 1, pass_x)
            arrived(R2, which, half)
            where(y < 3, lambda: send(slots[R2], R4, which, half, Y2, at(dy=1)))
            where(c == 1, lambda: send(slots[R2], R1, which, half, C1, at(dc=1)))

            def pass_y():
                arrived(VIA_Y, which, half)
                send(slots[VIA_Y], R4, which, half, YB2, at(dy=-1))

            where(y == 1, pass_y)

    halves(phase1)
    arrived(VIA_Z, 0, 1, LOWER)
    send(slots[VIA_Z], R128, 0, 1, ZM2, at(dz=-2), LOWER, 4)

    def near(half):
        for which in range(2):
            arrived(R1, which, half)
        sweep(half, lambda j: [level1(j), level2(j)])

    near(0)
    arrived(R64, 0, 0)
    send(slots[R64], R128, 0, 0, ZP, at(dz=2))
    near(1)
    arrived(R64, 0, 1)
    send(slots[R64], R128, 0, 1, ZP, at(dz=2), UPPER, 2)

    def phase3(half):
        arrived(R64, 1, half)
        for which in range(2):
            arrived(R16, which, half)
        sweep(half, lambda j: [level7(j), level5(j)])

    halves(phase3)

    def phase4(half):
        for which in range(2):
            arrived(R4, which, half)
        sweep(half, lambda j: [level0(j), level3(j)])

    halves(phase4)

    arrived(R128, 0, 0)
    arrived(R128, 1, 0)
    sweep(0, lambda j: [level8(j)], last=True)
    arrived(R128, 0, 1, UPPER, 2)
    arrived(R128, 0, 1, LOWER, 4)
    arrived(R128, 1, 1)
    sweep(1, lambda j: [level8(j)], last=True)

    for g in range(KV_HEADS):
        out_copy(g).wait()

    if comm:

        def sent(lane, which, half, rows=(0, 2 * BLOCK), sem=None):
            remote(own, R1, which, half, lane, at(dz=1), rows, sem).wait_send()

        for half in range(2):
            for which in range(2):
                for lane in (Z1, X1, Y1, C1, Z2):
                    sent(lane, which, half)
                for condition, lane in (
                    (x < 3, X2), (x == 2, XB), (x == 1, XB2), (y < 3, Y2), (y == 2, YB), (y == 1, YB2),
                ):
                    where(condition, lambda: sent(lane, which, half))
            sent(ZM, 1, half)
            sent(ZM2, 1, half)
        sent(ZM, 0, 1, LOWER)
        sent(ZM2, 0, 1, LOWER, 4)
        sent(ZP, 0, 0)
        sent(ZP, 0, 1, UPPER, 2)


def body(queries, keys, values, pattern, keep, comm=True):
    rows, width = queries.shape
    kv = pltpu.VMEM(keys.shape, keys.dtype)
    return pl.pallas_call(
        functools.partial(kernel, comm),
        out_shape=jax.ShapeDtypeStruct((rows, width), queries.dtype),
        in_specs=[pl.BlockSpec(memory_space=pl.ANY)] * 5,
        out_specs=pl.BlockSpec(memory_space=pl.ANY),
        scratch_shapes=[kv] * (2 * SLOTS + 2)
        + [
            pltpu.VMEM((rows, width), queries.dtype),
            pltpu.VMEM((rows, width), queries.dtype),
            pltpu.VMEM((rows, width), queries.dtype),
            pltpu.VMEM((2 * KV_HEADS, GROUP * BLOCK, HEAD), jnp.float32),
            pltpu.VMEM((2 * KV_HEADS, GROUP * BLOCK, HEAD), jnp.float32),
            pltpu.VMEM((2 * KV_HEADS, GROUP * BLOCK, HEAD), jnp.float32),
            pltpu.VMEM((pattern.shape[1], HEAD), jnp.int32),
            pltpu.VMEM((keep.shape[1], HEAD), jnp.int32),
            pltpu.VMEM((2 * LEVELS, BLOCK, HEAD), jnp.bfloat16),
            pltpu.VMEM((2 * LEVELS, 8, HEAD), jnp.float32),
            pltpu.SemaphoreType.DMA((5,)),
            pltpu.SemaphoreType.DMA((KV_HEADS,)),
            pltpu.SemaphoreType.DMA((14, PIECES + 1)),
            pltpu.SemaphoreType.DMA((SLOTS, PIECES + 1)),
        ],
        compiler_params=pltpu.CompilerParams(
            vmem_limit_bytes=63 * 1024 * 1024,
            **(dict(collective_id=0, has_side_effects=True) if comm else {}),
        ),
        name="butterfly_attention",
    )(queries, keys, values, pattern.T, keep.T)


def solution(mesh):
    return jax.shard_map(
        body,
        mesh=mesh,
        in_specs=(
            P(("seq", "head"), None),
            P(("seq", "head"), None),
            P(("seq", "head"), None),
            P(),
            P(),
        ),
        out_specs=P(("seq", "head"), None),
        check_vma=False,
    )
```

time: 138 us -> 90.9 us (0.66)
  the two profiles are of different devices: /device:TPU:32 before, /device:TPU:8 now
where the time goes in v2:
time: 90.9 us; the launch traced here: 90.8 us
  Pallas kernels  86.1 us (95%)
  local copies, waits for them, and re-layouts  4.64 us (5%)
    pallas_call x1, Pallas kernels, body(): pl.pallas_call(functools.partial(kernel, comm), out_shape=jax.ShapeDtypeS...  86.1 us
    unnamed x1, local copies, waits for them, and re-layouts  4.64 us

profile of v2, /device:TPU:8, one launch (start us, length us, event | category | flops | bytes accessed | tf_op | source)
XLA Modules:
  0.0 90.8 jit_solution(12548815748205517778)
XLA Ops:
  0.0 86.1 %butterfly_attention.1 = bf16[256,8192]{1,0:T(8,128)(2,1)} custom-call(bf16[256,8192]{1,0:T(8,128)(2,1)} %q_hbm.1, bf16[256,1024]{1,0:T(8,128)(2,1)} %k_hbm.1, bf16[256,1024]{1,0:T(8,128)(2,1)} %v_hbm.1, s32[16,512]{1,0:T(8,128)} %bitcast.2, s32[16,512]{1,0:T(8,128)} %bitcast.3), custom_call_target="tpu_custom_call" | custom-call | tf_op jit(solution)/shard_map/butterfly_attention/pallas_call | solution.py:352
  86.1 4.6 %copy.7 = bf16[256,8192]{1,0:T(8,128)(2,1)} copy(bf16[256,8192]{1,0:T(8,128)(2,1)} %butterfly_attention.1) | data formatting | bytes 8388608

commit v3 on v2

--- a/solution.py
+++ b/solution.py
@@ -30,12 +30,12 @@
     return pair[which].at[pl.ds(rows[0], rows[1]), columns]
 
 
-UPPER, LOWER = (0, BLOCK), (BLOCK, BLOCK)
+UPPER, LOWER = (0, 208), (208, 48)
 
 
 def kernel(comm, q_hbm, k_hbm, v_hbm, pattern_hbm, keep_hbm, out_hbm, *scratch):
     buffers = scratch[: 2 * SLOTS + 2]
-    (q, q_rest, out, acc, mass, peak, pattern, keep, choice, blind, load_sem, out_sem, send_sem, recv_sem) = scratch[2 * SLOTS + 2 :]
+    (q, q_rest, out, acc, peak, pattern, keep, first_table, second_table, none_table, load_sem, out_sem, send_sem, recv_sem) = scratch[2 * SLOTS + 2 :]
     own_hbm = (k_hbm, v_hbm)
     own = (buffers[0], buffers[1])
     slots = [(buffers[2 + 2 * i], buffers[3 + 2 * i]) for i in range(SLOTS)]
@@ -104,9 +104,8 @@
                 where(x < 3, lambda: send(own_hbm, R8, which, half, X1, at(dx=1)))
                 where(y < 3, lambda: send(own_hbm, R2, which, half, Y1, at(dy=1)))
                 where(c == 0, lambda: send(own_hbm, R1, which, half, C1, at(dc=1)))
-                if which == 1:
-                    send(own_hbm, VIA_Z, 1, half, ZM, at(dz=-2))
-        send(own_hbm, VIA_Z, 0, 1, ZM, at(dz=-2), LOWER)
+            send(own_hbm, VIA_Z, 1, half, ZM, at(dz=-2))
+            send(own_hbm, VIA_Z, 0, half, ZM, at(dz=-2), LOWER)
 
     for load in loads:
         load.wait()
@@ -122,11 +121,15 @@
                 found = jnp.where(here, table, 0.0)
                 return jnp.sum(jnp.sum(found, axis=1, keepdims=True), axis=0, keepdims=True)
 
-            if level >= 1:
-                base = (2 * (me - 2 ** (level - 1))).astype(jnp.float32)
-                block = jnp.clip(entry(blocks) - base, 0.0, 1.0)
-                choice[j * LEVELS + level] = jnp.broadcast_to(block, (BLOCK, HEAD)).astype(jnp.bfloat16)
-            blind[j * LEVELS + level] = jnp.broadcast_to((entry(kept) - 1.0) * -NEG, (8, HEAD))
+            base = (2 * (me - max(1, 2**level // 2))).astype(jnp.float32)
+            second = jnp.clip(entry(blocks) - base, 0.0, 1.0)
+            used = entry(kept)
+            if level == 0:
+                second = jnp.zeros_like(second)
+            for table, value in (
+                (first_table, used * (1.0 - second)), (second_table, used * second), (none_table, 1.0 - used),
+            ):
+                table[j * LEVELS + level] = jnp.broadcast_to(value, (BLOCK, HEAD)).astype(jnp.bfloat16)
 
     def queries_of(item, first):
         j, g, t = item
@@ -147,16 +150,27 @@
     def gathered(j, g, sources):
         columns = pl.ds(pl.multiple_of(g * HEAD, HEAD), HEAD)
 
-        def taken(ref, block, level):
-            if block is not None:
-                return ref[pl.ds(block * BLOCK, BLOCK), columns]
-            first_block, second_block = (ref[pl.ds(i * BLOCK, BLOCK), columns] for i in range(2))
-            second = choice[j * LEVELS + level]
-            return first_block * (1 - second) + second_block * second
-
-        keys, values = (
-            [taken(pair[i], block, level) for pair, block, level in sources] for i in range(2)
-        )
+        anchor = jnp.broadcast_to(own[0][pl.ds(j * BLOCK, 1), columns], (BLOCK, HEAD))
+        keys, values = [], []
+        for pair, block, level in sources:
+            key, value = (
+                [ref[pl.ds(i * BLOCK, BLOCK), columns] for i in (range(2) if block is None else (block,))]
+                for ref in pair
+            )
+            if level is None:
+                keys.append(key[0])
+                values.append(jnp.concatenate([value[0], jnp.ones_like(value[0])], 1))
+                continue
+            table = j * LEVELS + level
+            one, none = first_table[table], none_table[table]
+            total_key, total_value = key[0] * one + anchor * none, value[0] * one
+            ones = one
+            if block is None:
+                two = second_table[table]
+                total_key, total_value = total_key + key[1] * two, total_value + value[1] * two
+                ones = one + two
+            keys.append(total_key)
+            values.append(jnp.concatenate([total_value, ones], 1))
         keys = jnp.concatenate(keys, 0) if len(keys) > 1 else keys[0]
         values = jnp.concatenate(values, 0) if len(values) > 1 else values[0]
         return jnp.concatenate([keys, keys], 1), values
@@ -174,12 +188,10 @@
         parts = []
         for i, level in enumerate(levels):
             part = scores[:, i * BLOCK : (i + 1) * BLOCK]
-            if first:
+            if level is None:
                 token = lax.broadcasted_iota(jnp.int32, part.shape, 0) % BLOCK
                 key = lax.broadcasted_iota(jnp.int32, part.shape, 1)
                 part = jnp.where(key <= token, part, NEG)
-            else:
-                part = part + blind[j * LEVELS + level][:1]
             parts.append(part)
         top = functools.reduce(jnp.maximum, parts)
         top = jnp.max(top, axis=1, keepdims=True)
@@ -187,23 +199,19 @@
         if not first:
             before = peak[unit, tile]
             top = jnp.maximum(before, top)
-        weights = [jnp.exp2(part - top) for part in parts]
-        added = functools.reduce(jnp.add, weights)
-        weights = [weight.astype(jnp.bfloat16) for weight in weights]
+        weights = [jnp.exp2(part - top).astype(jnp.bfloat16) for part in parts]
         weights = jnp.concatenate(weights, 1) if len(weights) > 1 else weights[0]
         total = jnp.dot(weights, values, preferred_element_type=jnp.float32)
         if not first:
             fade = jnp.exp2(before - top)
-            total = total + acc[unit, tile] * fade
-            added = added + mass[unit, tile] * fade
+            total = total + acc[unit, tile] * jnp.concatenate([fade, fade], 1)
         if last:
-            result = (total / jnp.sum(added, axis=1, keepdims=True)).astype(jnp.bfloat16)
+            result = (total[:, :HEAD] / total[:, HEAD:]).astype(jnp.bfloat16)
             for r in range(TILE):
                 columns = pl.ds(pl.multiple_of((g * GROUP + t * TILE + r) * HEAD, HEAD), HEAD)
                 out[pl.ds(j * BLOCK, BLOCK), columns] = result[r * BLOCK : (r + 1) * BLOCK]
         else:
             acc[unit, tile] = total
-            mass[unit, tile] = added
             peak[unit, tile] = top
 
     def out_copy(g):
@@ -217,6 +225,8 @@
                 g = half * HALF + i * WIDE + g
                 for j in range(2):
                     sources = sources_of(j)
+                    if not sources:
+                        continue
                     keys, values = gathered(j, g, sources)
                     levels = [level for _, _, level in sources]
                     for t in range(GROUP // TILE):
@@ -241,9 +251,6 @@
     level5, level6 = level_source(5, R16), level_source(6, R32)
     level7, level8 = level_source(7, R64), level_source(8, R128)
 
-    def level0(j):
-        return (slots[R1], 1, 0) if j == 0 else (own, 0, 0)
-
     def halves(phase):
         def step(half, carry):
             phase(half)
@@ -251,7 +258,10 @@
 
         lax.fori_loop(0, 2, step, 0)
 
-    halves(lambda half: sweep(half, lambda j: [(own, j, 0)], first=True))
+    def diagonal(j):
+        return [(own, j, None)] + [(own, 0, 0)] * j
+
+    halves(lambda half: sweep(half, diagonal, first=True))
 
     def phase1(half):
         for which in range(2):
@@ -265,7 +275,11 @@
             where(y == 2, lambda: send(slots[R8], VIA_Y, which, half, YB, at(dy=-1)))
         arrived(VIA_Z, 1, half)
         send(slots[VIA_Z], R128, 1, half, ZM2, at(dz=-2))
+        arrived(VIA_Z, 0, half, LOWER)
+        send(slots[VIA_Z], R128, 0, half, ZM2, at(dz=-2), LOWER, 4 + half)
         sweep(half, lambda j: [level6(j), level4(j)])
+
+    def near(half):
         for which in range(2):
 
             def pass_x():
@@ -283,44 +297,41 @@
 
             where(y == 1, pass_y)
 
-    halves(phase1)
-    arrived(VIA_Z, 0, 1, LOWER)
-    send(slots[VIA_Z], R128, 0, 1, ZM2, at(dz=-2), LOWER, 4)
-
-    def near(half):
         for which in range(2):
             arrived(R1, which, half)
         sweep(half, lambda j: [level1(j), level2(j)])
 
-    near(0)
-    arrived(R64, 0, 0)
-    send(slots[R64], R128, 0, 0, ZP, at(dz=2))
-    near(1)
-    arrived(R64, 0, 1)
-    send(slots[R64], R128, 0, 1, ZP, at(dz=2), UPPER, 2)
-
-    def phase3(half):
+    def far(half):
+        arrived(R64, 0, half)
+        send(slots[R64], R128, 0, half, ZP, at(dz=2), UPPER)
         arrived(R64, 1, half)
         for which in range(2):
             arrived(R16, which, half)
         sweep(half, lambda j: [level7(j), level5(j)])
 
-    halves(phase3)
-
-    def phase4(half):
+    def middle(half):
         for which in range(2):
             arrived(R4, which, half)
-        sweep(half, lambda j: [level0(j), level3(j)])
-
-    halves(phase4)
-
-    arrived(R128, 0, 0)
-    arrived(R128, 1, 0)
-    sweep(0, lambda j: [level8(j)], last=True)
-    arrived(R128, 0, 1, UPPER, 2)
-    arrived(R128, 0, 1, LOWER, 4)
-    arrived(R128, 1, 1)
-    sweep(1, lambda j: [level8(j)], last=True)
+        sweep(half, lambda j: [] if j else [(slots[R1], 1, 0), level3(j)])
+
+    late = jnp.where((x == 0) & (y <= 1), 1, 0) if comm else 0
+
+    def stage(i, carry):
+        pl.when(i < 2)(lambda: phase1(i))
+        pl.when((i == 0) | (i == 1 + late))(lambda: near(jnp.minimum(i, 1)))
+        pl.when((i == 2 - late) | (i == 3))(lambda: far(i // 3))
+        pl.when(i >= 2)(lambda: middle(i - 2))
+        return carry
+
+    lax.fori_loop(0, 4, stage, 0)
+
+    def phase3(half):
+        arrived(R128, 0, half, UPPER)
+        arrived(R128, 0, half, LOWER, 4 + half)
+        arrived(R128, 1, half)
+        sweep(half, lambda j: [level8(j)] + [level3(j)] * j, last=True)
+
+    halves(phase3)
 
     for g in range(KV_HEADS):
         out_copy(g).wait()
@@ -338,18 +349,53 @@
                     (x < 3, X2), (x == 2, XB), (x == 1, XB2), (y < 3, Y2), (y == 2, YB), (y == 1, YB2),
                 ):
                     where(condition, lambda: sent(lane, which, half))
-            sent(ZM, 1, half)
-            sent(ZM2, 1, half)
-        sent(ZM, 0, 1, LOWER)
-        sent(ZM2, 0, 1, LOWER, 4)
-        sent(ZP, 0, 0)
-        sent(ZP, 0, 1, UPPER, 2)
+            for lane in (ZM, ZM2):
+                sent(lane, 1, half)
+            sent(ZM, 0, half, LOWER)
+            sent(ZM2, 0, half, LOWER, 4 + half)
+            sent(ZP, 0, half, UPPER)
+
+
+def copy_kernel(source, target, held, in_sem, out_sem):
+    chunks, rows = held.shape[0], held.shape[1]
+
+    def read(i):
+        return pltpu.make_async_copy(source.at[pl.ds(i * rows, rows)], held.at[i], in_sem.at[i])
+
+    def write(i):
+        return pltpu.make_async_copy(held.at[i], target.at[pl.ds(i * rows, rows)], out_sem.at[i])
+
+    for i in range(chunks):
+        read(i).start()
+    for i in range(chunks):
+        read(i).wait()
+        write(i).start()
+    for i in range(chunks):
+        write(i).wait()
+
+
+def copied(array):
+    rows, width = array.shape
+    chunks = 16
+    return pl.pallas_call(
+        copy_kernel,
+        out_shape=jax.ShapeDtypeStruct(array.shape, array.dtype),
+        in_specs=[pl.BlockSpec(memory_space=pl.ANY)],
+        out_specs=pl.BlockSpec(memory_space=pl.ANY),
+        scratch_shapes=[
+            pltpu.VMEM((chunks, rows // chunks, width), array.dtype),
+            pltpu.SemaphoreType.DMA((chunks,)),
+            pltpu.SemaphoreType.DMA((chunks,)),
+        ],
+        compiler_params=pltpu.CompilerParams(vmem_limit_bytes=63 * 1024 * 1024),
+        name="copy_out",
+    )(array)
 
 
 def body(queries, keys, values, pattern, keep, comm=True):
     rows, width = queries.shape
     kv = pltpu.VMEM(keys.shape, keys.dtype)
-    return pl.pallas_call(
+    result = pl.pallas_call(
         functools.partial(kernel, comm),
         out_shape=jax.ShapeDtypeStruct((rows, width), queries.dtype),
         in_specs=[pl.BlockSpec(memory_space=pl.ANY)] * 5,
@@ -359,17 +405,17 @@
             pltpu.VMEM((rows, width), queries.dtype),
             pltpu.VMEM((rows, width), queries.dtype),
             pltpu.VMEM((rows, width), queries.dtype),
-            pltpu.VMEM((2 * KV_HEADS, GROUP * BLOCK, HEAD), jnp.float32),
-            pltpu.VMEM((2 * KV_HEADS, GROUP * BLOCK, HEAD), jnp.float32),
+            pltpu.VMEM((2 * KV_HEADS, GROUP * BLOCK, 2 * HEAD), jnp.float32),
             pltpu.VMEM((2 * KV_HEADS, GROUP * BLOCK, HEAD), jnp.float32),
             pltpu.VMEM((pattern.shape[1], HEAD), jnp.int32),
             pltpu.VMEM((keep.shape[1], HEAD), jnp.int32),
             pltpu.VMEM((2 * LEVELS, BLOCK, HEAD), jnp.bfloat16),
-            pltpu.VMEM((2 * LEVELS, 8, HEAD), jnp.float32),
+            pltpu.VMEM((2 * LEVELS, BLOCK, HEAD), jnp.bfloat16),
+            pltpu.VMEM((2 * LEVELS, BLOCK, HEAD), jnp.bfloat16),
             pltpu.SemaphoreType.DMA((5,)),
             pltpu.SemaphoreType.DMA((KV_HEADS,)),
-            pltpu.SemaphoreType.DMA((14, PIECES + 1)),
-            pltpu.SemaphoreType.DMA((SLOTS, PIECES + 1)),
+            pltpu.SemaphoreType.DMA((14, PIECES + 2)),
+            pltpu.SemaphoreType.DMA((SLOTS, PIECES + 2)),
         ],
         compiler_params=pltpu.CompilerParams(
             vmem_limit_bytes=63 * 1024 * 1024,
@@ -377,6 +423,7 @@
         ),
         name="butterfly_attention",
     )(queries, keys, values, pattern.T, keep.T)
+    return copied(result)
 
 
 def solution(mesh):

time: 90.9 us -> 85.1 us (0.936)
  local copies, waits for them, and re-layouts: 4.64 us -> 0 us
  Pallas kernels: 86.1 us -> 84.9 us
    pallas_call x1, Pallas kernels: 86.1 us -> 81.1 us  [body(): pl.pallas_call(functools.partial(kernel, comm), out_shape=jax.ShapeDtypeS...]
    unnamed x1 -> x0, local copies, waits for them, and re-layouts: 4.64 us -> none
    pallas_call x0 -> x1, Pallas kernels: none -> 3.85 us  [copied(): pl.pallas_call(copy_kernel, out_shape=jax.ShapeDtypeStruct(array.shape, a...]
where the time goes in v3:
time: 85.1 us; the launch traced here: 84.9 us
  Pallas kernels  84.9 us (100%)
    pallas_call x1, Pallas kernels, body(): pl.pallas_call(functools.partial(kernel, comm), out_shape=jax.ShapeDtypeS...  81.1 us
    pallas_call x1, Pallas kernels, copied(): pl.pallas_call(copy_kernel, out_shape=jax.ShapeDtypeStruct(array.shape, a...  3.85 us

profile of v3, /device:TPU:8, one launch (start us, length us, event | category | flops | bytes accessed | tf_op | source)
XLA Modules:
  0.0 84.9 jit_solution(6672121086586314258)
XLA Ops:
  0.0 81.1 %butterfly_attention.1.source = bf16[256,8192]{1,0:T(8,128)(2,1)} custom-call(bf16[256,8192]{1,0:T(8,128)(2,1)} %q_hbm.1, bf16[256,1024]{1,0:T(8,128)(2,1)} %k_hbm.1, bf16[256,1024]{1,0:T(8,128)(2,1)} %v_hbm.1, s32[16,512]{1,0:T(8,128)} %bitcast.2, s32[16,512]{1,0:T(8,128)} %bitcast.3), custom_call_target="tpu_custom_call" | custom-call | tf_op jit(solution)/shard_map/butterfly_attention/pallas_call | solution.py:398
  81.1 3.9 %copy_out.1 = bf16[256,8192]{1,0:T(8,128)(2,1)} custom-call(bf16[256,8192]{1,0:T(8,128)(2,1)} %butterfly_attention.1.source), custom_call_target="tpu_custom_call" | custom-call | tf_op jit(solution)/shard_map/copy_out/pallas_call | solution.py:380

commit v4 on v3

--- a/solution.py
+++ b/solution.py
@@ -273,11 +273,11 @@
             where(x < 3, lambda: send(slots[R8], R16, which, half, X2, at(dx=1)))
             where(y == 3, lambda: send(slots[R8], R2, which, half, Y1, at(dy=1)))
             where(y == 2, lambda: send(slots[R8], VIA_Y, which, half, YB, at(dy=-1)))
+        sweep(half, lambda j: [level6(j), level4(j)])
         arrived(VIA_Z, 1, half)
         send(slots[VIA_Z], R128, 1, half, ZM2, at(dz=-2))
         arrived(VIA_Z, 0, half, LOWER)
         send(slots[VIA_Z], R128, 0, half, ZM2, at(dz=-2), LOWER, 4 + half)
-        sweep(half, lambda j: [level6(j), level4(j)])
 
     def near(half):
         for which in range(2):

time: 85.1 us -> 84.2 us (0.989)
  no operation moved by 1% of the time
where the time goes in v4:
time: 84.2 us; the launch traced here: 84.1 us
  Pallas kernels  84.1 us (100%)
    pallas_call x1, Pallas kernels, body(): pl.pallas_call(functools.partial(kernel, comm), out_shape=jax.ShapeDtypeS...  80.3 us
    pallas_call x1, Pallas kernels, copied(): pl.pallas_call(copy_kernel, out_shape=jax.ShapeDtypeStruct(array.shape, a...  3.85 us

profile of v4, /device:TPU:8, one launch (start us, length us, event | category | flops | bytes accessed | tf_op | source)
XLA Modules:
  0.0 84.1 jit_solution(9456091216178057865)
XLA Ops:
  0.0 80.3 %butterfly_attention.1.source = bf16[256,8192]{1,0:T(8,128)(2,1)} custom-call(bf16[256,8192]{1,0:T(8,128)(2,1)} %q_hbm.1, bf16[256,1024]{1,0:T(8,128)(2,1)} %k_hbm.1, bf16[256,1024]{1,0:T(8,128)(2,1)} %v_hbm.1, s32[16,512]{1,0:T(8,128)} %bitcast.2, s32[16,512]{1,0:T(8,128)} %bitcast.3), custom_call_target="tpu_custom_call" | custom-call | tf_op jit(solution)/shard_map/butterfly_attention/pallas_call | solution.py:398
  80.3 3.9 %copy_out.1 = bf16[256,8192]{1,0:T(8,128)(2,1)} custom-call(bf16[256,8192]{1,0:T(8,128)(2,1)} %butterfly_attention.1.source), custom_call_target="tpu_custom_call" | custom-call | tf_op jit(solution)/shard_map/copy_out/pallas_call | solution.py:380

commit v5 on v4

--- a/solution.py
+++ b/solution.py
@@ -30,7 +30,7 @@
     return pair[which].at[pl.ds(rows[0], rows[1]), columns]
 
 
-UPPER, LOWER = (0, 208), (208, 48)
+UPPER, LOWER = (0, 192), (192, 64)
 
 
 def kernel(comm, q_hbm, k_hbm, v_hbm, pattern_hbm, keep_hbm, out_hbm, *scratch):

time: 84.2 us -> 82.7 us (0.982)
  Pallas kernels: 84.1 us -> 82.6 us
    pallas_call x1, Pallas kernels: 80.3 us -> 78.7 us  [body(): pl.pallas_call(functools.partial(kernel, comm), out_shape=jax.ShapeDtypeS...]
where the time goes in v5:
time: 82.7 us; the launch traced here: 82.6 us
  Pallas kernels  82.6 us (100%)
    pallas_call x1, Pallas kernels, body(): pl.pallas_call(functools.partial(kernel, comm), out_shape=jax.ShapeDtypeS...  78.7 us
    pallas_call x1, Pallas kernels, copied(): pl.pallas_call(copy_kernel, out_shape=jax.ShapeDtypeStruct(array.shape, a...  3.85 us

profile of v5, /device:TPU:8, one launch (start us, length us, event | category | flops | bytes accessed | tf_op | source)
XLA Modules:
  0.0 82.6 jit_solution(9652705091597491465)
XLA Ops:
  0.0 78.7 %butterfly_attention.1.source = bf16[256,8192]{1,0:T(8,128)(2,1)} custom-call(bf16[256,8192]{1,0:T(8,128)(2,1)} %q_hbm.1, bf16[256,1024]{1,0:T(8,128)(2,1)} %k_hbm.1, bf16[256,1024]{1,0:T(8,128)(2,1)} %v_hbm.1, s32[16,512]{1,0:T(8,128)} %bitcast.2, s32[16,512]{1,0:T(8,128)} %bitcast.3), custom_call_target="tpu_custom_call" | custom-call | tf_op jit(solution)/shard_map/butterfly_attention/pallas_call | solution.py:398
  78.7 3.9 %copy_out.1 = bf16[256,8192]{1,0:T(8,128)(2,1)} custom-call(bf16[256,8192]{1,0:T(8,128)(2,1)} %butterfly_attention.1.source), custom_call_target="tpu_custom_call" | custom-call | tf_op jit(solution)/shard_map/copy_out/pallas_call | solution.py:380
